TPU v7x, 128 devices: a whole 4x4x4 slice. The times are simulated.
128 devices in a mesh: gx: 8 (over x, core), gy: 16 (over z, y).
Axes of the slice: x: 4, y: 4, z: 4, core: 2. Of those that a mesh axis runs over, the one named last changes fastest.
Arguments:
- parent_fields: float32 [5, 4, 384, 6144], P(None, None, 'gx', 'gy'), may hold values from -6 to 6
- parent_velocity: float32 [2, 4, 384, 6144], P(None, None, 'gx', 'gy'), may hold values from -0.3 to 0.3
- parent_mixing: float32 [4, 384, 6144], P(None, 'gx', 'gy'), may hold values from 0.01 to 0.1
- nest_fields: float32 [5, 4, 384, 6144], P(None, None, 'gx', 'gy'), may hold values from -6 to 6
- nest_velocity: float32 [2, 4, 384, 6144], P(None, None, 'gx', 'gy'), may hold values from -0.3 to 0.3
- nest_mixing: float32 [4, 384, 6144], P(None, 'gx', 'gy'), may hold values from 0.01 to 0.1
- nest_anchor: int32 [2], replicated, may hold values from 1 to 3327, as said below
Outputs:
- parent_result: float32 [5, 4, 384, 6144], P(None, None, 'gx', 'gy')
- nest_result: float32 [5, 4, 384, 6144], P(None, None, 'gx', 'gy')
Inputs may be any that keep to these rules, and one draw needn't show every extreme that they name: `nest_anchor`: the row anchor is 1 to 254; the column anchor is 3073 to 3327, so the nest with a rim of one parent cell lies inside the parent grid.
All inputs are finite; a program needn't handle non-finite values.
Results may differ from a plain program's by a relative error of at most 0.00002.
Values sent between devices are 32-bit elements; how exact they have to be, the bound alone decides.
A program may use at most 192 MiB of HBM per device.

v0:
```python
import jax
import jax.numpy as jnp
from jax import lax
from jax.sharding import PartitionSpec as P

SUBSTEPS = 3
third = 1.0 / 3.0
two_thirds = 2.0 / 3.0
nudge_floor = 0.1
relax_width = 4.0


def shift_pairs(count, step):
    return [(i, i + step) for i in range(count) if 0 <= i + step < count]


def neighbours(cells):
    rows = lax.axis_size("gx")
    cols = lax.axis_size("gy")
    western = lax.ppermute(cells[:, :, -1:, :], "gx", shift_pairs(rows, 1))
    eastern = lax.ppermute(cells[:, :, :1, :], "gx", shift_pairs(rows, -1))
    southern = lax.ppermute(cells[:, :, :, -1:], "gy", shift_pairs(cols, 1))
    northern = lax.ppermute(cells[:, :, :, :1], "gy", shift_pairs(cols, -1))
    return (western, eastern, southern, northern)


def update(values, halo, velocity, mixing):
    west_row, east_row, south_col, north_col = halo
    western = jnp.concatenate([west_row, values[:, :, :-1, :]], axis=2)
    eastern = jnp.concatenate([values[:, :, 1:, :], east_row], axis=2)
    southern = jnp.concatenate([south_col, values[:, :, :, :-1]], axis=3)
    northern = jnp.concatenate([values[:, :, :, 1:], north_col], axis=3)
    along_rows = velocity[0]
    along_columns = velocity[1]
    upwind = (
        jnp.maximum(along_rows, 0.0) * (values - western)
        + jnp.minimum(along_rows, 0.0) * (eastern - values)
        + jnp.maximum(along_columns, 0.0) * (values - southern)
        + jnp.minimum(along_columns, 0.0) * (northern - values)
    )
    return values - upwind + mixing * (eastern + western + northern + southern - 4.0 * values)


def refine_rows(block):
    lower = block[:, :, :-2]
    centre = block[:, :, 1:-1]
    upper = block[:, :, 2:]
    stacked = jnp.stack(
        (third * lower + two_thirds * centre, centre, two_thirds * centre + third * upper), axis=3
    )
    extent = centre.shape
    return stacked.reshape(extent[0], extent[1], 3 * extent[2], extent[3])


def refine_columns(block):
    lower = block[:, :, :, :-2]
    centre = block[:, :, :, 1:-1]
    upper = block[:, :, :, 2:]
    stacked = jnp.stack(
        (third * lower + two_thirds * centre, centre, two_thirds * centre + third * upper), axis=4
    )
    extent = centre.shape
    return stacked.reshape(extent[0], extent[1], extent[2], 3 * extent[3])


def block_mean(state):
    extent = state.shape
    grouped = state.reshape(extent[0], extent[1], extent[2] // 3, 3, extent[3] // 3, 3)
    return jnp.sum(grouped, axis=(3, 5)) / 9.0


def relax_weight(row_global, column_global, total_rows, total_columns):
    row_distance = jnp.minimum(row_global, total_rows - 1 - row_global)
    column_distance = jnp.minimum(column_global, total_columns - 1 - column_global)
    distance = jnp.minimum(row_distance[:, None], column_distance[None, :]).astype(jnp.float32)
    return nudge_floor + (1.0 - nudge_floor) * jnp.exp(-distance / relax_width)


def within(positions, limit):
    return (positions >= 0) & (positions < limit)


def column_pairs(count, base, ratio, k, extra):
    pairs = []
    for m in range(count):
        j = ratio * m + k
        p = base + m + extra
        if j < count and p < count:
            pairs.append((p, j))
    return pairs


def per_device(
    parent_fields,
    parent_velocity,
    parent_mixing,
    nest_fields,
    nest_velocity,
    nest_mixing,
    nest_anchor,
):
    row_rank = lax.axis_index("gx")
    column_rank = lax.axis_index("gy")
    row_devices = lax.axis_size("gx")
    column_devices = lax.axis_size("gy")
    parent_rows = parent_fields.shape[2]
    parent_columns = parent_fields.shape[3]
    nest_rows = nest_fields.shape[2]
    nest_columns = nest_fields.shape[3]
    span_rows = nest_rows // 3
    span_columns = nest_columns // 3
    ratio = parent_columns // span_columns
    base = column_devices // 2
    base_column = base * parent_columns
    relay_rows = span_rows + 2
    relay_columns = span_columns + 2
    row_anchor = nest_anchor[0]
    column_anchor = nest_anchor[1]
    offset = column_anchor - 1 - base_column
    parent_next = update(parent_fields, neighbours(parent_fields), parent_velocity, parent_mixing)
    margin = parent_columns - span_columns
    wide = jnp.pad(parent_next, ((0, 0), (0, 0), (0, 0), (margin, margin)))
    relay_cols = None
    for k in range(ratio):
        for extra in (0, 1):
            if extra == 1 and k == 0:
                continue
            start = margin + span_columns * k + offset - extra * parent_columns
            piece = lax.dynamic_slice_in_dim(wide, start, relay_columns, axis=3)
            moved = lax.ppermute(piece, "gy", column_pairs(column_devices, base, ratio, k, extra))
            relay_cols = moved if relay_cols is None else relay_cols + moved
    padded = jnp.pad(relay_cols, ((0, 0), (0, 0), (relay_rows, relay_rows), (0, 0)))
    slots = []
    for target in range(row_devices):
        first = row_anchor - 1 + span_rows * target - parent_rows * row_rank
        first = jnp.clip(first, -relay_rows, parent_rows) + relay_rows
        slots.append(lax.dynamic_slice_in_dim(padded, first, relay_rows, axis=2))
    stacked = jnp.stack(slots, axis=0)
    relay = lax.psum_scatter(stacked, "gx", scatter_dimension=0, tiled=True)[0]
    forcing = refine_columns(refine_rows(relay))
    row_global = row_rank * nest_rows + jnp.arange(nest_rows, dtype=jnp.int32)
    column_global = column_rank * nest_columns + jnp.arange(nest_columns, dtype=jnp.int32)
    weight = relax_weight(
        row_global, column_global, row_devices * nest_rows, column_devices * nest_columns
    )
    state = nest_fields
    for substep in range(SUBSTEPS):
        moved = update(state, neighbours(state), nest_velocity, nest_mixing)
        state = moved + weight * (forcing - moved)
    coarse = block_mean(state)
    gathered = lax.all_gather(coarse, "gx", axis=2, tiled=True)
    total_span = row_devices * span_rows
    gathered = jnp.pad(gathered, ((0, 0), (0, 0), (parent_rows, parent_rows), (0, 0)))
    first = jnp.clip(parent_rows * row_rank - row_anchor, -parent_rows, total_span)
    strip = lax.dynamic_slice_in_dim(gathered, first + parent_rows, parent_rows, axis=2)
    pieces = []
    for extra in (1, 0):
        for k in range(ratio):
            if extra == 1 and k == 0:
                continue
            pairs = [(j, p) for p, j in column_pairs(column_devices, base, ratio, k, extra)]
            pieces.append(lax.ppermute(strip, "gy", pairs))
    joined = jnp.concatenate(pieces, axis=3)
    start = (ratio - 1) * span_columns - 1 - offset
    fed_back = lax.dynamic_slice_in_dim(joined, start, parent_columns, axis=3)
    relative_rows = row_rank * parent_rows + jnp.arange(parent_rows, dtype=jnp.int32) - row_anchor
    relative_columns = (
        column_rank * parent_columns + jnp.arange(parent_columns, dtype=jnp.int32) - column_anchor
    )
    rows_valid = within(relative_rows, total_span)
    columns_valid = within(relative_columns, column_devices * span_columns)
    covered = rows_valid[:, None] & columns_valid[None, :]
    parent_result = jnp.where(covered, fed_back, parent_next)
    return (parent_result, state)


def solution(mesh):
    placed = (
        P(None, None, "gx", "gy"),
        P(None, None, "gx", "gy"),
        P(None, "gx", "gy"),
        P(None, None, "gx", "gy"),
        P(None, None, "gx", "gy"),
        P(None, "gx", "gy"),
        P(),
    )
    return jax.shard_map(
        per_device,
        mesh=mesh,
        in_specs=placed,
        out_specs=(P(None, None, "gx", "gy"), P(None, None, "gx", "gy")),
        check_vma=False,
    )
```

profile of v0, /device:TPU:73, one launch (start us, length us, event | category | flops | bytes accessed | tf_op | source)
XLA Modules:
  0.0 439.8 jit_solution(16195591423806882408)
XLA Ops:
  9.6 3.2 collective-permute-start.6
  15.6 4.2 collective-permute-start.4
  45.4 4.0 multiply_add_fusion.3
  61.8 11.4 %collective-permute-done.10 = f32[5,4,48,130]{3,2,1,0:T(8,128)S(1)} collective-permute-done((f32[5,4,48,130]{3,2,1,0:T(8,128)S(1)}, f32[5,4,48,130]{3,2,1,0:T(8,128)S(1)}, u32[]{:S(2)}, u32[]{:S(2)}) %collective-permute-start.10) | collective-permute-done | bytes 499232 | tf_op jit(solution)/shard_map/ppermute | solution.py:130
  73.2 8.7 %collective-permute-start.2 = (f32[5,4,48,1]{3,2,1,0:T(8,128)}, f32[5,4,48,1]{3,2,1,0:T(8,128)}, u32[]{:S(2)}, u32[]{:S(2)}) collective-permute-start(f32[5,4,48,1]{3,2,1,0:T(8,128)} %get-tuple-element.30), channel_id=1, source_target_pairs={{0,1},{1,2},{2,3},{3,4},{4,5},{5,6},{6,7},{7,8},{8,9},{9,10},{10,1... | collective-permute-start | bytes 11528 | tf_op jit(solution)/shard_map/ppermute | solution.py:22
  81.9 20.6 %collective-permute-start.3 = (f32[5,4,48,1]{3,2,1,0:T(8,128)}, f32[5,4,48,1]{3,2,1,0:T(8,128)}, u32[]{:S(2)}, u32[]{:S(2)}) collective-permute-start(f32[5,4,48,1]{3,2,1,0:T(8,128)} %get-tuple-element.31), channel_id=1, source_target_pairs={{1,0},{2,1},{3,2},{4,3},{5,4},{6,5},{7,6},{8,7},{9,8},{10,9},{11,1... | collective-permute-start | bytes 11528 | tf_op jit(solution)/shard_map/ppermute | solution.py:23
  102.6 5.0 %collective-permute-start = (f32[5,4,1,384]{3,1,2,0:T(4,128)}, f32[5,4,1,384]{3,1,2,0:T(4,128)}, u32[]{:S(2)}, u32[]{:S(2)}) collective-permute-start(f32[5,4,1,384]{3,1,2,0:T(4,128)} %copy.336), channel_id=1, source_target_pairs={{0,16},{16,32},{32,48},{48,64},{64,80},{80,96},{96,112},{1,17},{17... | collective-permute-start | bytes 92168 | tf_op jit(solution)/shard_map/ppermute | solution.py:20
  124.5 81.9 %all-reduce.6.cloned.1.call-done = f32[8,5,4,18,130]{4,2,3,1,0:T(4,128)} async-done(((f32[8,5,4,18,130]{4,2,3,1,0:T(4,128)}), f32[8,5,4,18,130]{4,2,3,1,0:T(4,128)}) %all-reduce.6.cloned.1.call-update) | async-done | bytes 1497616
  209.7 3.6 copy.317
  213.3 3.4 copy.318
  216.8 4.1 multiply_add_fusion.2
  221.4 3.1 collective-permute-start.15
  226.7 3.6 collective-permute-start.13
  230.4 2.8 collective-permute-start.14
  238.7 2.9 collective-permute-start.19
  241.5 3.1 collective-permute-start.20
  244.6 5.0 %collective-permute-start.17 = (f32[5,4,1,384]{3,1,2,0:T(4,128)S(1)}, f32[5,4,1,384]{3,1,2,0:T(4,128)S(1)}, u32[]{:S(2)}, u32[]{:S(2)}) collective-permute-start(f32[5,4,1,384]{3,1,2,0:T(4,128)S(1)} %copy.324), channel_id=1, source_target_pairs={{0,16},{16,32},{32,48},{48,64},{64,80},{80,96},{96,112},{1,17},{17... | collective-permute-start | bytes 92168 | tf_op jit(solution)/shard_map/ppermute | solution.py:20
  252.2 3.0 collective-permute-done.18
  257.1 60.9 %reshape.74 = f32[5,4,16,3,128,3]{5,4,3,2,1,0:T(8,128)} reshape(f32[5,4,48,384]{3,2,1,0:T(8,128)S(1)} %multiply_add_fusion) | data formatting | bytes 2949120 | tf_op jit(solution)/shard_map/reshape | solution.py:68
  318.0 20.5 %reduce_sum.9 = f32[5,4,16,128]{3,2,1,0:T(8,128)S(1)} reduce(f32[5,4,16,3,128,3]{5,4,3,2,1,0:T(8,128)} %reshape.74, f32[]{:T(128)} %constant.93.clone.1), dimensions={3,5}, to_apply=%region_1.2 | reduce | flops 327680 | bytes 1638404 | tf_op jit(solution)/shard_map/reduce_sum | solution.py:69
  339.9 32.5 %all-gather.2.cloned.1.call-done = f32[5,4,128,128]{3,1,0,2:T(4,128)} async-done(((f32[5,4,16,128]{3,1,0,2:T(4,128)}), f32[5,4,128,128]{3,1,0,2:T(4,128)}) %all-gather.2.cloned.1.call-update) | async-done | bytes 1310736 | tf_op jit(solution)/shard_map/all_gather | solution.py:151
  375.9 5.3 %collective-permute-start.23 = (f32[5,4,48,128]{3,2,1,0:T(8,128)S(1)}, f32[5,4,48,128]{3,2,1,0:T(8,128)S(1)}, u32[]{:S(2)}, u32[]{:S(2)}) collective-permute-start(f32[5,4,48,128]{3,2,1,0:T(8,128)S(1)} %copy.330), channel_id=1, source_target_pairs={{0,8},{3,9},{6,10},{9,11},{12,12},{15,13},{16,24},{19,25},{22,26},... | collective-permute-start | bytes 1474568 | tf_op jit(solution)/shard_map/ppermute | solution.py:162
  384.5 35.7 %collective-permute-done.21 = f32[5,4,48,128]{3,2,1,0:T(8,128)S(1)} collective-permute-done((f32[5,4,48,128]{3,2,1,0:T(8,128)S(1)}, f32[5,4,48,128]{3,2,1,0:T(8,128)S(1)}, u32[]{:S(2)}, u32[]{:S(2)}) %collective-permute-start.21) | collective-permute-done | bytes 491552 | tf_op jit(solution)/shard_map/ppermute | solution.py:162
  420.4 10.8 %collective-permute-done.25 = f32[5,4,48,128]{3,2,1,0:T(8,128)S(1)} collective-permute-done((f32[5,4,48,128]{3,2,1,0:T(8,128)S(1)}, f32[5,4,48,128]{3,2,1,0:T(8,128)S(1)}, u32[]{:S(2)}, u32[]{:S(2)}) %collective-permute-start.25) | collective-permute-done | bytes 491552 | tf_op jit(solution)/shard_map/ppermute | solution.py:162
  (137 shorter events, 73.2 us)
Async XLA Ops:
  7.2 199.3 %all-reduce.6.cloned.1.call-start = ((), (), s32[]{:S(2)}) async-start(), calls=%async_computation.1 | async-start | bytes 5898240
  9.6 35.7 %collective-permute-start.6 = (f32[5,4,48,1]{3,2,1,0:T(8,128)}, f32[5,4,48,1]{3,2,1,0:T(8,128)}, u32[]{:S(2)}, u32[]{:S(2)}) collective-permute-start(f32[5,4,48,1]{3,2,1,0:T(8,128)} %get-tuple-element.43), channel_id=1, source_target_pairs={{0,1},{1,2},{2,3},{3,4},{4,5},{5,6},{6,7},{7,8},{8,9},{9,10},{10,1... | collective-permute-start | bytes 11528 | tf_op jit(solution)/shard_map/ppermute | solution.py:22
  12.8 32.5 %collective-permute-start.7 = (f32[5,4,48,1]{3,2,1,0:T(8,128)}, f32[5,4,48,1]{3,2,1,0:T(8,128)}, u32[]{:S(2)}, u32[]{:S(2)}) collective-permute-start(f32[5,4,48,1]{3,2,1,0:T(8,128)} %get-tuple-element.44), channel_id=1, source_target_pairs={{1,0},{2,1},{3,2},{4,3},{5,4},{6,5},{7,6},{8,7},{9,8},{10,9},{11,1... | collective-permute-start | bytes 11528 | tf_op jit(solution)/shard_map/ppermute | solution.py:23
  15.6 28.2 %collective-permute-start.4 = (f32[5,4,1,384]{3,1,2,0:T(4,128)}, f32[5,4,1,384]{3,1,2,0:T(4,128)}, u32[]{:S(2)}, u32[]{:S(2)}) collective-permute-start(f32[5,4,1,384]{3,1,2,0:T(4,128)} %copy.338), channel_id=1, source_target_pairs={{0,16},{16,32},{32,48},{48,64},{64,80},{80,96},{96,112},{1,17},{17... | collective-permute-start | bytes 92168 | tf_op jit(solution)/shard_map/ppermute | solution.py:20
  20.4 24.1 %collective-permute-start.5 = (f32[5,4,1,384]{3,1,2,0:T(4,128)}, f32[5,4,1,384]{3,1,2,0:T(4,128)}, u32[]{:S(2)}, u32[]{:S(2)}) collective-permute-start(f32[5,4,1,384]{3,1,2,0:T(4,128)} %copy.339), channel_id=1, source_target_pairs={{16,0},{32,16},{48,32},{64,48},{80,64},{96,80},{112,96},{17,1},{33... | collective-permute-start | bytes 92168 | tf_op jit(solution)/shard_map/ppermute | solution.py:21
  50.8 22.4 %collective-permute-start.10 = (f32[5,4,48,130]{3,2,1,0:T(8,128)S(1)}, f32[5,4,48,130]{3,2,1,0:T(8,128)S(1)}, u32[]{:S(2)}, u32[]{:S(2)}) collective-permute-start(f32[5,4,48,130]{3,2,1,0:T(8,128)S(1)} %get-tuple-element.35), channel_id=1, source_target_pairs={{9,1},{10,4},{11,7},{12,10},{13,13},{25,17},{26,20},{27,23},{28,26... | collective-permute-start | bytes 1497608 | tf_op jit(solution)/shard_map/ppermute | solution.py:130
  53.0 29.0 %collective-permute-start.11 = (f32[5,4,48,130]{3,2,1,0:T(8,128)S(1)}, f32[5,4,48,130]{3,2,1,0:T(8,128)S(1)}, u32[]{:S(2)}, u32[]{:S(2)}) collective-permute-start(f32[5,4,48,130]{3,2,1,0:T(8,128)S(1)} %get-tuple-element.36), channel_id=1, source_target_pairs={{8,2},{9,5},{10,8},{11,11},{12,14},{24,18},{25,21},{26,24},{27,27}... | collective-permute-start | bytes 1497608 | tf_op jit(solution)/shard_map/ppermute | solution.py:130
  54.3 48.2 %collective-permute-start.12 = (f32[5,4,48,130]{3,2,1,0:T(8,128)S(1)}, f32[5,4,48,130]{3,2,1,0:T(8,128)S(1)}, u32[]{:S(2)}, u32[]{:S(2)}) collective-permute-start(f32[5,4,48,130]{3,2,1,0:T(8,128)S(1)} %get-tuple-element.37), channel_id=1, source_target_pairs={{9,2},{10,5},{11,8},{12,11},{13,14},{25,18},{26,21},{27,24},{28,27... | collective-permute-start | bytes 1497608 | tf_op jit(solution)/shard_map/ppermute | solution.py:130
  55.7 51.9 %collective-permute-start.8 = (f32[5,4,48,130]{3,2,1,0:T(8,128)S(1)}, f32[5,4,48,130]{3,2,1,0:T(8,128)S(1)}, u32[]{:S(2)}, u32[]{:S(2)}) collective-permute-start(f32[5,4,48,130]{3,2,1,0:T(8,128)S(1)} %get-tuple-element.38), channel_id=1, source_target_pairs={{8,0},{9,3},{10,6},{11,9},{12,12},{13,15},{24,16},{25,19},{26,22},... | collective-permute-start | bytes 1497608 | tf_op jit(solution)/shard_map/ppermute | solution.py:130
  57.6 52.0 %collective-permute-start.9 = (f32[5,4,48,130]{3,2,1,0:T(8,128)S(1)}, f32[5,4,48,130]{3,2,1,0:T(8,128)S(1)}, u32[]{:S(2)}, u32[]{:S(2)}) collective-permute-start(f32[5,4,48,130]{3,2,1,0:T(8,128)S(1)} %get-tuple-element.34), channel_id=1, source_target_pairs={{8,1},{9,4},{10,7},{11,10},{12,13},{24,17},{25,20},{26,23},{27,26}... | collective-permute-start | bytes 1497608 | tf_op jit(solution)/shard_map/ppermute | solution.py:130
  73.2 143.6 %collective-permute-start.2 = (f32[5,4,48,1]{3,2,1,0:T(8,128)}, f32[5,4,48,1]{3,2,1,0:T(8,128)}, u32[]{:S(2)}, u32[]{:S(2)}) collective-permute-start(f32[5,4,48,1]{3,2,1,0:T(8,128)} %get-tuple-element.30), channel_id=1, source_target_pairs={{0,1},{1,2},{2,3},{3,4},{4,5},{5,6},{6,7},{7,8},{8,9},{9,10},{10,1... | collective-permute-start | bytes 11528 | tf_op jit(solution)/shard_map/ppermute | solution.py:22
  81.9 134.8 %collective-permute-start.3 = (f32[5,4,48,1]{3,2,1,0:T(8,128)}, f32[5,4,48,1]{3,2,1,0:T(8,128)}, u32[]{:S(2)}, u32[]{:S(2)}) collective-permute-start(f32[5,4,48,1]{3,2,1,0:T(8,128)} %get-tuple-element.31), channel_id=1, source_target_pairs={{1,0},{2,1},{3,2},{4,3},{5,4},{6,5},{7,6},{8,7},{9,8},{10,9},{11,1... | collective-permute-start | bytes 11528 | tf_op jit(solution)/shard_map/ppermute | solution.py:23
  102.6 19.2 %collective-permute-start = (f32[5,4,1,384]{3,1,2,0:T(4,128)}, f32[5,4,1,384]{3,1,2,0:T(4,128)}, u32[]{:S(2)}, u32[]{:S(2)}) collective-permute-start(f32[5,4,1,384]{3,1,2,0:T(4,128)} %copy.336), channel_id=1, source_target_pairs={{0,16},{16,32},{32,48},{48,64},{64,80},{80,96},{96,112},{1,17},{17... | collective-permute-start | bytes 92168 | tf_op jit(solution)/shard_map/ppermute | solution.py:20
  107.6 15.5 %collective-permute-start.1 = (f32[5,4,1,384]{3,1,2,0:T(4,128)}, f32[5,4,1,384]{3,1,2,0:T(4,128)}, u32[]{:S(2)}, u32[]{:S(2)}) collective-permute-start(f32[5,4,1,384]{3,1,2,0:T(4,128)} %copy.337), channel_id=1, source_target_pairs={{16,0},{32,16},{48,32},{64,48},{80,64},{96,80},{112,96},{17,1},{33... | collective-permute-start | bytes 92168 | tf_op jit(solution)/shard_map/ppermute | solution.py:21
  118.0 254.4 %all-gather.2.cloned.1.call-start = ((), (), s32[]{:S(2)}) async-start(), calls=%async_computation | async-start | bytes 1474560 | tf_op jit(solution)/shard_map/all_gather | solution.py:151
  221.4 14.6 %collective-permute-start.15 = (f32[5,4,48,1]{3,2,1,0:T(8,128)S(1)}, f32[5,4,48,1]{3,2,1,0:T(8,128)S(1)}, u32[]{:S(2)}, u32[]{:S(2)}) collective-permute-start(f32[5,4,48,1]{3,2,1,0:T(8,128)S(1)} %get-tuple-element.22), channel_id=1, source_target_pairs={{0,1},{1,2},{2,3},{3,4},{4,5},{5,6},{6,7},{7,8},{8,9},{9,10},{10,1... | collective-permute-start | bytes 11528 | tf_op jit(solution)/shard_map/ppermute | solution.py:22
  224.5 11.8 %collective-permute-start.16 = (f32[5,4,48,1]{3,2,1,0:T(8,128)S(1)}, f32[5,4,48,1]{3,2,1,0:T(8,128)S(1)}, u32[]{:S(2)}, u32[]{:S(2)}) collective-permute-start(f32[5,4,48,1]{3,2,1,0:T(8,128)S(1)} %get-tuple-element.23), channel_id=1, source_target_pairs={{1,0},{2,1},{3,2},{4,3},{5,4},{6,5},{7,6},{8,7},{9,8},{10,9},{11,1... | collective-permute-start | bytes 11528 | tf_op jit(solution)/shard_map/ppermute | solution.py:23
  238.7 16.6 %collective-permute-start.19 = (f32[5,4,48,1]{3,2,1,0:T(8,128)S(1)}, f32[5,4,48,1]{3,2,1,0:T(8,128)S(1)}, u32[]{:S(2)}, u32[]{:S(2)}) collective-permute-start(f32[5,4,48,1]{3,2,1,0:T(8,128)S(1)} %get-tuple-element.14), channel_id=1, source_target_pairs={{0,1},{1,2},{2,3},{3,4},{4,5},{5,6},{6,7},{7,8},{8,9},{9,10},{10,1... | collective-permute-start | bytes 11528 | tf_op jit(solution)/shard_map/ppermute | solution.py:22
  241.5 13.7 %collective-permute-start.20 = (f32[5,4,48,1]{3,2,1,0:T(8,128)S(1)}, f32[5,4,48,1]{3,2,1,0:T(8,128)S(1)}, u32[]{:S(2)}, u32[]{:S(2)}) collective-permute-start(f32[5,4,48,1]{3,2,1,0:T(8,128)S(1)} %get-tuple-element.15), channel_id=1, source_target_pairs={{1,0},{2,1},{3,2},{4,3},{5,4},{6,5},{7,6},{8,7},{9,8},{10,9},{11,1... | collective-permute-start | bytes 11528 | tf_op jit(solution)/shard_map/ppermute | solution.py:23
  372.6 47.6 %collective-permute-start.21 = (f32[5,4,48,128]{3,2,1,0:T(8,128)S(1)}, f32[5,4,48,128]{3,2,1,0:T(8,128)S(1)}, u32[]{:S(2)}, u32[]{:S(2)}) collective-permute-start(f32[5,4,48,128]{3,2,1,0:T(8,128)S(1)} %copy.330), channel_id=1, source_target_pairs={{1,9},{4,10},{7,11},{10,12},{13,13},{17,25},{20,26},{23,27},{26,28... | collective-permute-start | bytes 1474568 | tf_op jit(solution)/shard_map/ppermute | solution.py:162
  373.9 46.4 %collective-permute-start.22 = (f32[5,4,48,128]{3,2,1,0:T(8,128)S(1)}, f32[5,4,48,128]{3,2,1,0:T(8,128)S(1)}, u32[]{:S(2)}, u32[]{:S(2)}) collective-permute-start(f32[5,4,48,128]{3,2,1,0:T(8,128)S(1)} %copy.330), channel_id=1, source_target_pairs={{2,9},{5,10},{8,11},{11,12},{14,13},{18,25},{21,26},{24,27},{27,28... | collective-permute-start | bytes 1474568 | tf_op jit(solution)/shard_map/ppermute | solution.py:162
  375.9 44.5 %collective-permute-start.23 = (f32[5,4,48,128]{3,2,1,0:T(8,128)S(1)}, f32[5,4,48,128]{3,2,1,0:T(8,128)S(1)}, u32[]{:S(2)}, u32[]{:S(2)}) collective-permute-start(f32[5,4,48,128]{3,2,1,0:T(8,128)S(1)} %copy.330), channel_id=1, source_target_pairs={{0,8},{3,9},{6,10},{9,11},{12,12},{15,13},{16,24},{19,25},{22,26},... | collective-permute-start | bytes 1474568 | tf_op jit(solution)/shard_map/ppermute | solution.py:162
  381.8 38.6 %collective-permute-start.24 = (f32[5,4,48,128]{3,2,1,0:T(8,128)S(1)}, f32[5,4,48,128]{3,2,1,0:T(8,128)S(1)}, u32[]{:S(2)}, u32[]{:S(2)}) collective-permute-start(f32[5,4,48,128]{3,2,1,0:T(8,128)S(1)} %copy.330), channel_id=1, source_target_pairs={{1,8},{4,9},{7,10},{10,11},{13,12},{17,24},{20,25},{23,26},{26,27}... | collective-permute-start | bytes 1474568 | tf_op jit(solution)/shard_map/ppermute | solution.py:162
  383.2 48.1 %collective-permute-start.25 = (f32[5,4,48,128]{3,2,1,0:T(8,128)S(1)}, f32[5,4,48,128]{3,2,1,0:T(8,128)S(1)}, u32[]{:S(2)}, u32[]{:S(2)}) collective-permute-start(f32[5,4,48,128]{3,2,1,0:T(8,128)S(1)} %copy.330), channel_id=1, source_target_pairs={{2,8},{5,9},{8,10},{11,11},{14,12},{18,24},{21,25},{24,26},{27,27}... | collective-permute-start | bytes 1474568 | tf_op jit(solution)/shard_map/ppermute | solution.py:162
  (17 other events, 149.6 us)
Sparse Core Ops, SparseCore 0:
  118.2 88.2 all-reduce.5
  339.4 32.9 all-gather.1
where the time goes:
time: 441 us; the launch traced here: 440 us
  waiting for transfers between devices  178 us (40%)
  local copies, waits for them, and re-layouts  104 us (24%)
  starting transfers between devices  91.2 us (21%)
  other arithmetic  39.5 us (9%)
  between operations  27 us (6%)
    unnamed x3, waiting for transfers between devices  81.9 us
    reshape x1, local copies, waits for them, and re-layouts, block_mean(): state.reshape(extent[0], extent[1], extent[2] // 3, 3, extent[3] // 3, 3)  60.9 us
    ppermute x5, waiting for transfers between devices, per_device(): pieces.append(lax.ppermute(strip, 'gy', pairs))  46.6 us
    all_gather x1, waiting for transfers between devices, per_device(): gathered = lax.all_gather(coarse, 'gx', axis=2, tiled=True)  32.5 us
    ppermute x4, starting transfers between devices, neighbours(): northern = lax.ppermute(cells[:, :, :, :1], 'gy', shift_pairs(cols, -1))  28 us
    reduce_sum x1, other arithmetic, block_mean(): return jnp.sum(grouped, axis=(3, 5)) / 9.0  20.5 us
    ppermute x4, starting transfers between devices, neighbours(): southern = lax.ppermute(cells[:, :, :, -1:], 'gy', shift_pairs(cols, 1))  17.9 us
    ppermute x4, starting transfers between devices, neighbours(): western = lax.ppermute(cells[:, :, -1:, :], 'gx', shift_pairs(rows, 1))  17.9 us
  transfers between devices with their start and end apart: 28, of which 8 were waited for; matrix products, arithmetic and copies ran while one was open for 10% of the time, Pallas kernels for 0%

commit v1 on v0

--- a/solution.py
+++ b/solution.py
@@ -8,6 +8,11 @@
 two_thirds = 2.0 / 3.0
 nudge_floor = 0.1
 relax_width = 4.0
+
+
+def gather_by_exchange(x, axis, dim):
+    copies = jnp.concatenate([x] * lax.axis_size(axis), axis=dim)
+    return lax.all_to_all(copies, axis, dim, dim, tiled=True)
 
 
 def shift_pairs(count, step):
@@ -148,7 +153,7 @@
         moved = update(state, neighbours(state), nest_velocity, nest_mixing)
         state = moved + weight * (forcing - moved)
     coarse = block_mean(state)
-    gathered = lax.all_gather(coarse, "gx", axis=2, tiled=True)
+    gathered = gather_by_exchange(coarse, "gx", 2)
     total_span = row_devices * span_rows
     gathered = jnp.pad(gathered, ((0, 0), (0, 0), (parent_rows, parent_rows), (0, 0)))
     first = jnp.clip(parent_rows * row_rank - row_anchor, -parent_rows, total_span)

time: 441 us -> 439 us (level)
  waiting for transfers between devices: 178 us -> 162 us
  starting transfers between devices: 91.2 us -> 103 us
    all_gather x1 -> x0, waiting for transfers between devices: 32.5 us -> none  [per_device(): gathered = lax.all_gather(coarse, 'gx', axis=2, tiled=True)]
    all_to_all x0 -> x1, waiting for transfers between devices: none -> 17.3 us  [gather_by_exchange(): return lax.all_to_all(copies, axis, dim, dim, tiled=True)]
    all_to_all x0 -> x1, starting transfers between devices: none -> 11 us  [gather_by_exchange(): return lax.all_to_all(copies, axis, dim, dim, tiled=True)]
    unnamed x3 -> x2, waiting for transfers between devices: 81.9 us -> 82 us
where the time goes in v1:
time: 439 us; the launch traced here: 438 us
  waiting for transfers between devices  162 us (37%)
  local copies, waits for them, and re-layouts  106 us (24%)
  starting transfers between devices  103 us (23%)
  other arithmetic  39.6 us (9%)
  between operations  26.9 us (6%)
    unnamed x2, waiting for transfers between devices  82 us
    reshape x1, local copies, waits for them, and re-layouts, block_mean(): state.reshape(extent[0], extent[1], extent[2] // 3, 3, extent[3] // 3, 3)  60.9 us
    ppermute x5, waiting for transfers between devices, per_device(): pieces.append(lax.ppermute(strip, 'gy', pairs))  46.1 us
    ppermute x4, starting transfers between devices, neighbours(): northern = lax.ppermute(cells[:, :, :, :1], 'gy', shift_pairs(cols, -1))  28 us
    reduce_sum x1, other arithmetic, block_mean(): return jnp.sum(grouped, axis=(3, 5)) / 9.0  20.5 us
    ppermute x4, starting transfers between devices, neighbours(): southern = lax.ppermute(cells[:, :, :, -1:], 'gy', shift_pairs(cols, 1))  17.9 us
    ppermute x4, starting transfers between devices, neighbours(): western = lax.ppermute(cells[:, :, -1:, :], 'gx', shift_pairs(rows, 1))  17.9 us
    all_to_all x1, waiting for transfers between devices, gather_by_exchange(): return lax.all_to_all(copies, axis, dim, dim, tiled=True)  17.3 us
  transfers between devices with their start and end apart: 28, of which 8 were waited for; matrix products, arithmetic and copies ran while one was open for 10% of the time, Pallas kernels for 0%

profile of v1, /device:TPU:73, one launch (start us, length us, event | category | flops | bytes accessed | tf_op | source)
XLA Modules:
  0.0 437.8 jit_solution(13969954149878112049)
XLA Ops:
  9.6 3.2 collective-permute-start.6
  15.6 4.2 collective-permute-start.4
  45.2 4.0 multiply_add_fusion.3
  61.6 11.4 %collective-permute-done.10 = f32[5,4,48,130]{3,2,1,0:T(8,128)S(1)} collective-permute-done((f32[5,4,48,130]{3,2,1,0:T(8,128)S(1)}, f32[5,4,48,130]{3,2,1,0:T(8,128)S(1)}, u32[]{:S(2)}, u32[]{:S(2)}) %collective-permute-start.10) | collective-permute-done | bytes 499232 | tf_op jit(solution)/shard_map/ppermute | solution.py:135
  73.0 8.8 %collective-permute-start.2 = (f32[5,4,48,1]{3,2,1,0:T(8,128)}, f32[5,4,48,1]{3,2,1,0:T(8,128)}, u32[]{:S(2)}, u32[]{:S(2)}) collective-permute-start(f32[5,4,48,1]{3,2,1,0:T(8,128)} %get-tuple-element.32), channel_id=1, source_target_pairs={{0,1},{1,2},{2,3},{3,4},{4,5},{5,6},{6,7},{7,8},{8,9},{9,10},{10,1... | collective-permute-start | bytes 11528 | tf_op jit(solution)/shard_map/ppermute | solution.py:27
  81.8 20.6 %collective-permute-start.3 = (f32[5,4,48,1]{3,2,1,0:T(8,128)}, f32[5,4,48,1]{3,2,1,0:T(8,128)}, u32[]{:S(2)}, u32[]{:S(2)}) collective-permute-start(f32[5,4,48,1]{3,2,1,0:T(8,128)} %get-tuple-element.33), channel_id=1, source_target_pairs={{1,0},{2,1},{3,2},{4,3},{5,4},{6,5},{7,6},{8,7},{9,8},{10,9},{11,1... | collective-permute-start | bytes 11528 | tf_op jit(solution)/shard_map/ppermute | solution.py:28
  102.4 5.1 %collective-permute-start = (f32[5,4,1,384]{3,1,2,0:T(4,128)}, f32[5,4,1,384]{3,1,2,0:T(4,128)}, u32[]{:S(2)}, u32[]{:S(2)}) collective-permute-start(f32[5,4,1,384]{3,1,2,0:T(4,128)} %copy.445), channel_id=1, source_target_pairs={{0,16},{16,32},{32,48},{48,64},{64,80},{80,96},{96,112},{1,17},{17... | collective-permute-start | bytes 92168 | tf_op jit(solution)/shard_map/ppermute | solution.py:25
  124.3 82.0 %all-reduce.6.cloned.1.call-done = f32[8,5,4,18,130]{4,2,3,1,0:T(4,128)} async-done(((f32[8,5,4,18,130]{4,2,3,1,0:T(4,128)}), f32[8,5,4,18,130]{4,2,3,1,0:T(4,128)}) %all-reduce.6.cloned.1.call-update) | async-done | bytes 1497616
  209.5 3.6 copy.426
  213.1 3.4 copy.427
  216.5 4.1 multiply_add_fusion.2
  221.2 3.1 collective-permute-start.15
  226.5 3.6 collective-permute-start.13
  230.1 2.8 collective-permute-start.14
  238.4 2.9 collective-permute-start.19
  241.3 3.1 collective-permute-start.20
  244.4 5.0 %collective-permute-start.17 = (f32[5,4,1,384]{3,1,2,0:T(4,128)S(1)}, f32[5,4,1,384]{3,1,2,0:T(4,128)S(1)}, u32[]{:S(2)}, u32[]{:S(2)}) collective-permute-start(f32[5,4,1,384]{3,1,2,0:T(4,128)S(1)} %copy.433), channel_id=1, source_target_pairs={{0,16},{16,32},{32,48},{48,64},{64,80},{80,96},{96,112},{1,17},{17... | collective-permute-start | bytes 92168 | tf_op jit(solution)/shard_map/ppermute | solution.py:25
  257.9 60.9 %reshape.74 = f32[5,4,16,3,128,3]{5,4,3,2,1,0:T(8,128)} reshape(f32[5,4,48,384]{3,2,1,0:T(8,128)S(1)} %multiply_add_fusion) | data formatting | bytes 2949120 | tf_op jit(solution)/shard_map/reshape | solution.py:73
  318.9 20.5 %reduce_sum.9 = f32[5,4,16,128]{3,2,1,0:T(8,128)S(1)} reduce(f32[5,4,16,3,128,3]{5,4,3,2,1,0:T(8,128)} %reshape.74, f32[]{:T(128)} %constant.93.clone.1), dimensions={3,5}, to_apply=%region_1.2 | reduce | flops 327680 | bytes 1638404 | tf_op jit(solution)/shard_map/reduce_sum | solution.py:74
  341.5 11.0 %all-to-all-start = ((f32[5,4,128,128]{3,1,0,2:T(4,128)}), f32[5,4,128,128]{3,1,0,2:T(4,128)S(1)}, u32[]{:S(2)}, u32[]{:S(2)}) async-start(f32[5,4,128,128]{3,1,0,2:T(4,128)} %copy.438), calls=%async_computation | async-start | bytes 2621440 | tf_op jit(solution)/shard_map/all_to_all | solution.py:15
  353.1 17.3 %all-to-all-done = f32[5,4,128,128]{3,1,0,2:T(4,128)S(1)} async-done(((f32[5,4,128,128]{3,1,0,2:T(4,128)}), f32[5,4,128,128]{3,1,0,2:T(4,128)S(1)}, u32[]{:S(2)}, u32[]{:S(2)}) %all-to-all-start) | async-done | bytes 1310752 | tf_op jit(solution)/shard_map/all_to_all | solution.py:15
  373.9 5.8 %collective-permute-start.23 = (f32[5,4,48,128]{3,2,1,0:T(8,128)S(1)}, f32[5,4,48,128]{3,2,1,0:T(8,128)S(1)}, u32[]{:S(2)}, u32[]{:S(2)}) collective-permute-start(f32[5,4,48,128]{3,2,1,0:T(8,128)S(1)} %copy.439), channel_id=1, source_target_pairs={{0,8},{3,9},{6,10},{9,11},{12,12},{15,13},{16,24},{19,25},{22,26},... | collective-permute-start | bytes 1474568 | tf_op jit(solution)/shard_map/ppermute | solution.py:167
  383.0 34.5 %collective-permute-done.21 = f32[5,4,48,128]{3,2,1,0:T(8,128)S(1)} collective-permute-done((f32[5,4,48,128]{3,2,1,0:T(8,128)S(1)}, f32[5,4,48,128]{3,2,1,0:T(8,128)S(1)}, u32[]{:S(2)}, u32[]{:S(2)}) %collective-permute-start.21) | collective-permute-done | bytes 491552 | tf_op jit(solution)/shard_map/ppermute | solution.py:167
  417.7 11.6 %collective-permute-done.25 = f32[5,4,48,128]{3,2,1,0:T(8,128)S(1)} collective-permute-done((f32[5,4,48,128]{3,2,1,0:T(8,128)S(1)}, f32[5,4,48,128]{3,2,1,0:T(8,128)S(1)}, u32[]{:S(2)}, u32[]{:S(2)}) %collective-permute-start.25) | collective-permute-done | bytes 491552 | tf_op jit(solution)/shard_map/ppermute | solution.py:167
  (143 shorter events, 78.5 us)
Async XLA Ops:
  7.2 199.1 %all-reduce.6.cloned.1.call-start = ((), (), s32[]{:S(2)}) async-start(), calls=%async_computation.1 | async-start | bytes 5898240
  9.6 35.6 %collective-permute-start.6 = (f32[5,4,48,1]{3,2,1,0:T(8,128)}, f32[5,4,48,1]{3,2,1,0:T(8,128)}, u32[]{:S(2)}, u32[]{:S(2)}) collective-permute-start(f32[5,4,48,1]{3,2,1,0:T(8,128)} %get-tuple-element.45), channel_id=1, source_target_pairs={{0,1},{1,2},{2,3},{3,4},{4,5},{5,6},{6,7},{7,8},{8,9},{9,10},{10,1... | collective-permute-start | bytes 11528 | tf_op jit(solution)/shard_map/ppermute | solution.py:27
  12.8 32.4 %collective-permute-start.7 = (f32[5,4,48,1]{3,2,1,0:T(8,128)}, f32[5,4,48,1]{3,2,1,0:T(8,128)}, u32[]{:S(2)}, u32[]{:S(2)}) collective-permute-start(f32[5,4,48,1]{3,2,1,0:T(8,128)} %get-tuple-element.46), channel_id=1, source_target_pairs={{1,0},{2,1},{3,2},{4,3},{5,4},{6,5},{7,6},{8,7},{9,8},{10,9},{11,1... | collective-permute-start | bytes 11528 | tf_op jit(solution)/shard_map/ppermute | solution.py:28
  15.6 28.1 %collective-permute-start.4 = (f32[5,4,1,384]{3,1,2,0:T(4,128)}, f32[5,4,1,384]{3,1,2,0:T(4,128)}, u32[]{:S(2)}, u32[]{:S(2)}) collective-permute-start(f32[5,4,1,384]{3,1,2,0:T(4,128)} %copy.447), channel_id=1, source_target_pairs={{0,16},{16,32},{32,48},{48,64},{64,80},{80,96},{96,112},{1,17},{17... | collective-permute-start | bytes 92168 | tf_op jit(solution)/shard_map/ppermute | solution.py:25
  20.4 24.0 %collective-permute-start.5 = (f32[5,4,1,384]{3,1,2,0:T(4,128)}, f32[5,4,1,384]{3,1,2,0:T(4,128)}, u32[]{:S(2)}, u32[]{:S(2)}) collective-permute-start(f32[5,4,1,384]{3,1,2,0:T(4,128)} %copy.448), channel_id=1, source_target_pairs={{16,0},{32,16},{48,32},{64,48},{80,64},{96,80},{112,96},{17,1},{33... | collective-permute-start | bytes 92168 | tf_op jit(solution)/shard_map/ppermute | solution.py:26
  50.7 22.3 %collective-permute-start.10 = (f32[5,4,48,130]{3,2,1,0:T(8,128)S(1)}, f32[5,4,48,130]{3,2,1,0:T(8,128)S(1)}, u32[]{:S(2)}, u32[]{:S(2)}) collective-permute-start(f32[5,4,48,130]{3,2,1,0:T(8,128)S(1)} %get-tuple-element.37), channel_id=1, source_target_pairs={{9,1},{10,4},{11,7},{12,10},{13,13},{25,17},{26,20},{27,23},{28,26... | collective-permute-start | bytes 1497608 | tf_op jit(solution)/shard_map/ppermute | solution.py:135
  52.8 29.0 %collective-permute-start.11 = (f32[5,4,48,130]{3,2,1,0:T(8,128)S(1)}, f32[5,4,48,130]{3,2,1,0:T(8,128)S(1)}, u32[]{:S(2)}, u32[]{:S(2)}) collective-permute-start(f32[5,4,48,130]{3,2,1,0:T(8,128)S(1)} %get-tuple-element.38), channel_id=1, source_target_pairs={{8,2},{9,5},{10,8},{11,11},{12,14},{24,18},{25,21},{26,24},{27,27}... | collective-permute-start | bytes 1497608 | tf_op jit(solution)/shard_map/ppermute | solution.py:135
  54.2 48.2 %collective-permute-start.12 = (f32[5,4,48,130]{3,2,1,0:T(8,128)S(1)}, f32[5,4,48,130]{3,2,1,0:T(8,128)S(1)}, u32[]{:S(2)}, u32[]{:S(2)}) collective-permute-start(f32[5,4,48,130]{3,2,1,0:T(8,128)S(1)} %get-tuple-element.39), channel_id=1, source_target_pairs={{9,2},{10,5},{11,8},{12,11},{13,14},{25,18},{26,21},{27,24},{28,27... | collective-permute-start | bytes 1497608 | tf_op jit(solution)/shard_map/ppermute | solution.py:135
  55.5 52.0 %collective-permute-start.8 = (f32[5,4,48,130]{3,2,1,0:T(8,128)S(1)}, f32[5,4,48,130]{3,2,1,0:T(8,128)S(1)}, u32[]{:S(2)}, u32[]{:S(2)}) collective-permute-start(f32[5,4,48,130]{3,2,1,0:T(8,128)S(1)} %get-tuple-element.40), channel_id=1, source_target_pairs={{8,0},{9,3},{10,6},{11,9},{12,12},{13,15},{24,16},{25,19},{26,22},... | collective-permute-start | bytes 1497608 | tf_op jit(solution)/shard_map/ppermute | solution.py:135
  57.5 52.2 %collective-permute-start.9 = (f32[5,4,48,130]{3,2,1,0:T(8,128)S(1)}, f32[5,4,48,130]{3,2,1,0:T(8,128)S(1)}, u32[]{:S(2)}, u32[]{:S(2)}) collective-permute-start(f32[5,4,48,130]{3,2,1,0:T(8,128)S(1)} %get-tuple-element.36), channel_id=1, source_target_pairs={{8,1},{9,4},{10,7},{11,10},{12,13},{24,17},{25,20},{26,23},{27,26}... | collective-permute-start | bytes 1497608 | tf_op jit(solution)/shard_map/ppermute | solution.py:135
  73.0 143.5 %collective-permute-start.2 = (f32[5,4,48,1]{3,2,1,0:T(8,128)}, f32[5,4,48,1]{3,2,1,0:T(8,128)}, u32[]{:S(2)}, u32[]{:S(2)}) collective-permute-start(f32[5,4,48,1]{3,2,1,0:T(8,128)} %get-tuple-element.32), channel_id=1, source_target_pairs={{0,1},{1,2},{2,3},{3,4},{4,5},{5,6},{6,7},{7,8},{8,9},{9,10},{10,1... | collective-permute-start | bytes 11528 | tf_op jit(solution)/shard_map/ppermute | solution.py:27
  81.8 134.7 %collective-permute-start.3 = (f32[5,4,48,1]{3,2,1,0:T(8,128)}, f32[5,4,48,1]{3,2,1,0:T(8,128)}, u32[]{:S(2)}, u32[]{:S(2)}) collective-permute-start(f32[5,4,48,1]{3,2,1,0:T(8,128)} %get-tuple-element.33), channel_id=1, source_target_pairs={{1,0},{2,1},{3,2},{4,3},{5,4},{6,5},{7,6},{8,7},{9,8},{10,9},{11,1... | collective-permute-start | bytes 11528 | tf_op jit(solution)/shard_map/ppermute | solution.py:28
  102.4 19.1 %collective-permute-start = (f32[5,4,1,384]{3,1,2,0:T(4,128)}, f32[5,4,1,384]{3,1,2,0:T(4,128)}, u32[]{:S(2)}, u32[]{:S(2)}) collective-permute-start(f32[5,4,1,384]{3,1,2,0:T(4,128)} %copy.445), channel_id=1, source_target_pairs={{0,16},{16,32},{32,48},{48,64},{64,80},{80,96},{96,112},{1,17},{17... | collective-permute-start | bytes 92168 | tf_op jit(solution)/shard_map/ppermute | solution.py:25
  107.5 15.4 %collective-permute-start.1 = (f32[5,4,1,384]{3,1,2,0:T(4,128)}, f32[5,4,1,384]{3,1,2,0:T(4,128)}, u32[]{:S(2)}, u32[]{:S(2)}) collective-permute-start(f32[5,4,1,384]{3,1,2,0:T(4,128)} %copy.446), channel_id=1, source_target_pairs={{16,0},{32,16},{48,32},{64,48},{80,64},{96,80},{112,96},{17,1},{33... | collective-permute-start | bytes 92168 | tf_op jit(solution)/shard_map/ppermute | solution.py:26
  221.2 14.6 %collective-permute-start.15 = (f32[5,4,48,1]{3,2,1,0:T(8,128)S(1)}, f32[5,4,48,1]{3,2,1,0:T(8,128)S(1)}, u32[]{:S(2)}, u32[]{:S(2)}) collective-permute-start(f32[5,4,48,1]{3,2,1,0:T(8,128)S(1)} %get-tuple-element.24), channel_id=1, source_target_pairs={{0,1},{1,2},{2,3},{3,4},{4,5},{5,6},{6,7},{7,8},{8,9},{9,10},{10,1... | collective-permute-start | bytes 11528 | tf_op jit(solution)/shard_map/ppermute | solution.py:27
  224.3 11.8 %collective-permute-start.16 = (f32[5,4,48,1]{3,2,1,0:T(8,128)S(1)}, f32[5,4,48,1]{3,2,1,0:T(8,128)S(1)}, u32[]{:S(2)}, u32[]{:S(2)}) collective-permute-start(f32[5,4,48,1]{3,2,1,0:T(8,128)S(1)} %get-tuple-element.25), channel_id=1, source_target_pairs={{1,0},{2,1},{3,2},{4,3},{5,4},{6,5},{7,6},{8,7},{9,8},{10,9},{11,1... | collective-permute-start | bytes 11528 | tf_op jit(solution)/shard_map/ppermute | solution.py:28
  238.4 16.6 %collective-permute-start.19 = (f32[5,4,48,1]{3,2,1,0:T(8,128)S(1)}, f32[5,4,48,1]{3,2,1,0:T(8,128)S(1)}, u32[]{:S(2)}, u32[]{:S(2)}) collective-permute-start(f32[5,4,48,1]{3,2,1,0:T(8,128)S(1)} %get-tuple-element.16), channel_id=1, source_target_pairs={{0,1},{1,2},{2,3},{3,4},{4,5},{5,6},{6,7},{7,8},{8,9},{9,10},{10,1... | collective-permute-start | bytes 11528 | tf_op jit(solution)/shard_map/ppermute | solution.py:27
  241.3 13.7 %collective-permute-start.20 = (f32[5,4,48,1]{3,2,1,0:T(8,128)S(1)}, f32[5,4,48,1]{3,2,1,0:T(8,128)S(1)}, u32[]{:S(2)}, u32[]{:S(2)}) collective-permute-start(f32[5,4,48,1]{3,2,1,0:T(8,128)S(1)} %get-tuple-element.17), channel_id=1, source_target_pairs={{1,0},{2,1},{3,2},{4,3},{5,4},{6,5},{7,6},{8,7},{9,8},{10,9},{11,1... | collective-permute-start | bytes 11528 | tf_op jit(solution)/shard_map/ppermute | solution.py:28
  341.5 28.9 %all-to-all-start = ((f32[5,4,128,128]{3,1,0,2:T(4,128)}), f32[5,4,128,128]{3,1,0,2:T(4,128)S(1)}, u32[]{:S(2)}, u32[]{:S(2)}) async-start(f32[5,4,128,128]{3,1,0,2:T(4,128)} %copy.438), calls=%async_computation | async-start | bytes 2621440 | tf_op jit(solution)/shard_map/all_to_all | solution.py:15
  370.6 46.9 %collective-permute-start.21 = (f32[5,4,48,128]{3,2,1,0:T(8,128)S(1)}, f32[5,4,48,128]{3,2,1,0:T(8,128)S(1)}, u32[]{:S(2)}, u32[]{:S(2)}) collective-permute-start(f32[5,4,48,128]{3,2,1,0:T(8,128)S(1)} %copy.439), channel_id=1, source_target_pairs={{1,9},{4,10},{7,11},{10,12},{13,13},{17,25},{20,26},{23,27},{26,28... | collective-permute-start | bytes 1474568 | tf_op jit(solution)/shard_map/ppermute | solution.py:167
  371.9 45.6 %collective-permute-start.22 = (f32[5,4,48,128]{3,2,1,0:T(8,128)S(1)}, f32[5,4,48,128]{3,2,1,0:T(8,128)S(1)}, u32[]{:S(2)}, u32[]{:S(2)}) collective-permute-start(f32[5,4,48,128]{3,2,1,0:T(8,128)S(1)} %copy.439), channel_id=1, source_target_pairs={{2,9},{5,10},{8,11},{11,12},{14,13},{18,25},{21,26},{24,27},{27,28... | collective-permute-start | bytes 1474568 | tf_op jit(solution)/shard_map/ppermute | solution.py:167
  373.9 43.8 %collective-permute-start.23 = (f32[5,4,48,128]{3,2,1,0:T(8,128)S(1)}, f32[5,4,48,128]{3,2,1,0:T(8,128)S(1)}, u32[]{:S(2)}, u32[]{:S(2)}) collective-permute-start(f32[5,4,48,128]{3,2,1,0:T(8,128)S(1)} %copy.439), channel_id=1, source_target_pairs={{0,8},{3,9},{6,10},{9,11},{12,12},{15,13},{16,24},{19,25},{22,26},... | collective-permute-start | bytes 1474568 | tf_op jit(solution)/shard_map/ppermute | solution.py:167
  380.3 37.3 %collective-permute-start.24 = (f32[5,4,48,128]{3,2,1,0:T(8,128)S(1)}, f32[5,4,48,128]{3,2,1,0:T(8,128)S(1)}, u32[]{:S(2)}, u32[]{:S(2)}) collective-permute-start(f32[5,4,48,128]{3,2,1,0:T(8,128)S(1)} %copy.439), channel_id=1, source_target_pairs={{1,8},{4,9},{7,10},{10,11},{13,12},{17,24},{20,25},{23,26},{26,27}... | collective-permute-start | bytes 1474568 | tf_op jit(solution)/shard_map/ppermute | solution.py:167
  381.7 47.6 %collective-permute-start.25 = (f32[5,4,48,128]{3,2,1,0:T(8,128)S(1)}, f32[5,4,48,128]{3,2,1,0:T(8,128)S(1)}, u32[]{:S(2)}, u32[]{:S(2)}) collective-permute-start(f32[5,4,48,128]{3,2,1,0:T(8,128)S(1)} %copy.439), channel_id=1, source_target_pairs={{2,8},{5,9},{8,10},{11,11},{14,12},{18,24},{21,25},{24,26},{27,27}... | collective-permute-start | bytes 1474568 | tf_op jit(solution)/shard_map/ppermute | solution.py:167
  (17 other events, 90.7 us)
Sparse Core Ops, SparseCore 0:
  118.2 88.0 all-reduce.5
